TPU v7x, 32 devices: a whole 2x2x4 slice. The times are simulated.
32 devices in a mesh: tm: 4 (over z), chan: 8 (over y, x, core).
Axes of the slice: x: 2, y: 2, z: 4, core: 2. Of those that a mesh axis runs over, the one named last changes fastest.
Arguments:
- voltages: bfloat16 [512, 1024, 1024], P('chan', None, 'tm'), may hold values from -4 to 4
- exponents: int32 [512, 16, 4], P('chan', None, 'tm'), may hold values from -2 to 2
- gain_real: float32 [512, 1024], P(None, 'chan'), may hold values from 0.1 to 1.9
- gain_imag: float32 [512, 1024], P(None, 'chan'), may hold values from -1.5 to 1.5
- delays: float32 [512, 256], replicated, may hold values from -8 to 8
- filter_taps: float32 [4, 1024], replicated, may hold values from -3 to 3
Outputs:
- beam_series: bfloat16 [256, 1024, 1024], P('chan', None, 'tm')
All inputs are finite; a program needn't handle non-finite values.
Results may differ from a plain program's by a relative error of at most 0.0062.
Values may be sent and summed in bfloat16 or wider, within the bound.
A program may use at most 320 MiB of HBM per device.

v0:
```python
import math

import jax
import jax.numpy as jnp
from jax import lax
from jax.sharding import PartitionSpec as P

C = 1024


TWO_PI = 6.283185307179586


def from_behind(block, axis, distance):
    devices = range(lax.axis_size(axis))
    route = [(i - distance, i) for i in devices if i - distance in devices]
    return lax.ppermute(block, axis, route)


def inverse_tables(length):
    row_index = lax.broadcasted_iota(jnp.int32, (length, length), 0)
    col_index = lax.broadcasted_iota(jnp.int32, (length, length), 1)
    phases = TWO_PI / length * (row_index * col_index % length).astype(jnp.float32)
    normalizer = 1.0 / math.sqrt(length)
    cosine_table = (jnp.cos(phases) * normalizer).astype(jnp.bfloat16)
    sine_table = (jnp.sin(phases) * normalizer).astype(jnp.bfloat16)
    return (cosine_table, sine_table)


def beam_weights(gain_real, gain_imag, delays, chan_start):
    local_count = gain_real.shape[1]
    stations = delays.shape[0]
    channel = (chan_start + lax.broadcasted_iota(jnp.int32, (local_count,), 0)).astype(jnp.float32)
    frequency = (channel + 0.5) / C - 0.5
    turns = TWO_PI * frequency
    phases = turns[:, None, None] * jnp.transpose(delays)[None, :, :]
    cosines = jnp.cos(phases)
    sines = jnp.sin(phases)
    real_gain = jnp.transpose(gain_real)[:, None, :]
    imag_gain = jnp.transpose(gain_imag)[:, None, :]
    scale_factor = 1.0 / math.sqrt(stations)
    weight_real = (real_gain * cosines + imag_gain * sines) * scale_factor
    weight_imag = (imag_gain * cosines - real_gain * sines) * scale_factor
    return jnp.concatenate([weight_real, weight_imag], axis=1).astype(jnp.bfloat16)


def form_beams(weights, received):
    stations = received.shape[0]
    local_count = received.shape[1]
    frame_count = received.shape[3]
    flattened = received.reshape(stations, local_count, 2 * frame_count)
    product = jnp.einsum("cos,sck->cok", weights, flattened, preferred_element_type=jnp.float32)
    beam_count = weights.shape[1] // 2
    real_part = product[:, :beam_count, :frame_count] - product[:, beam_count:, frame_count:]
    imag_part = product[:, :beam_count, frame_count:] + product[:, beam_count:, :frame_count]
    return jnp.stack([real_part, imag_part], axis=2).astype(jnp.bfloat16)


def synthesize(cosine_table, sine_table, spectra):
    channels = spectra.shape[0]
    beams_local = spectra.shape[1]
    frame_count = spectra.shape[3]
    flattened = spectra.reshape(channels, beams_local, 2 * frame_count)
    cosine_part = jnp.einsum(
        "cn,cbk->bnk", cosine_table, flattened, preferred_element_type=jnp.float32
    )
    sine_part = jnp.einsum("cn,cbk->bnk", sine_table, flattened, preferred_element_type=jnp.float32)
    real_part = cosine_part[:, :, :frame_count] - sine_part[:, :, frame_count:]
    imag_part = sine_part[:, :, :frame_count] + cosine_part[:, :, frame_count:]
    return jnp.stack([real_part, imag_part], axis=2)


def apply_taps(filter_taps, extended, frame_count):
    tail_length = filter_taps.shape[0] - 1
    running = jnp.zeros(extended.shape[:3] + (frame_count,), jnp.float32)
    for tap_index in range(filter_taps.shape[0]):
        begin = tail_length - tap_index
        running = (
            running
            + filter_taps[tap_index][None, :, None, None]
            * extended[:, :, :, begin : begin + frame_count]
        )
    return running


def per_device(voltages, exponents, gain_real, gain_imag, delays, filter_taps):
    channels = voltages.shape[1]
    frame_count = voltages.shape[2] // 2
    block_width = channels // exponents.shape[1]
    factor = jnp.repeat(jnp.exp2(exponents.astype(jnp.float32)), block_width, axis=1).astype(
        jnp.bfloat16
    )
    scaled = voltages * factor
    local_count = gain_real.shape[1]
    weights = beam_weights(gain_real, gain_imag, delays, lax.axis_index("chan") * local_count)
    received = lax.all_to_all(scaled, "chan", split_axis=1, concat_axis=0, tiled=True)
    beamed = form_beams(weights, received.reshape(received.shape[0], local_count, 2, frame_count))
    spectra = lax.all_to_all(beamed, "chan", split_axis=1, concat_axis=0, tiled=True)
    cosine_table, sine_table = inverse_tables(channels)
    signal = synthesize(cosine_table, sine_table, spectra)
    tail_length = filter_taps.shape[0] - 1
    zeros_front = jnp.zeros(signal.shape[:3] + (tail_length,), jnp.float32)
    local_out = apply_taps(filter_taps, jnp.concatenate([zeros_front, signal], axis=3), frame_count)
    outgoing = apply_taps(
        filter_taps,
        jnp.concatenate([signal[:, :, :, frame_count - tail_length :], zeros_front], axis=3),
        tail_length,
    )
    incoming = from_behind(outgoing, "tm", 1)
    output = jnp.concatenate(
        [local_out[:, :, :, :tail_length] + incoming, local_out[:, :, :, tail_length:]], axis=3
    )
    return output.reshape(output.shape[0], channels, 2 * frame_count).astype(jnp.bfloat16)


def solution(mesh):
    placed = (
        P("chan", None, "tm"),
        P("chan", None, "tm"),
        P(None, "chan"),
        P(None, "chan"),
        P(),
        P(),
    )
    return jax.shard_map(
        per_device, mesh=mesh, in_specs=placed, out_specs=P("chan", None, "tm"), check_vma=False
    )
```

profile of v0, /device:TPU:0, one launch (start us, length us, event | category | flops | bytes accessed | tf_op | source)
XLA Modules:
  0.0 1023.4 jit_solution(9505893554731898784)
XLA Ops:
  0.8 29.8 %copy_multiply_fusion = bf16[64,1024,256]{2,0,1:T(8,128)(2,1)} fusion(bf16[64,1024,256]{2,1,0:T(8,128)(2,1)} %param.6, bf16[64,1024]{0,1:T(8,128)(2,1)S(1)} %bitcast.55), kind=kLoop, calls=%fused_computation.19 | loop fusion | flops 16777216 | bytes 67239936 | tf_op jit(solution)/shard_map/mul | solution.py:93
  30.6 7.5 all-to-all-start
  38.7 257.1 %fusion.6 = (bf16[128,256,512]{2,1,0:T(8,128)(2,1)}, bf16[128,256,512]{2,1,0:T(8,128)(2,1)}) fusion(f32[128,512]{1,0:T(8,128)S(1)} %copy.34, f32[256,512]{1,0:T(8,128)S(1)} %copy.33, f32[128]{0:T(128)S(1)} %add_multiply_fusion, f32[128,512]{1,0:T(8,128)S(1)} %copy.32), kind=kLoop, calls=%fused_computation.8 | loop fusion | flops 184549376 | bytes 68157952 | tf_op jit(solution)/shard_map/convert.7
  295.8 106.7 %all-to-all-done = bf16[64,1024,256]{2,0,1:T(8,128)(2,1)} async-done(((bf16[64,1024,256]{2,0,1:T(8,128)(2,1)}), bf16[64,1024,256]{2,0,1:T(8,128)(2,1)}, u32[]{:S(2)}, u32[]{:S(2)}) %all-to-all-start) | async-done | bytes 33554464 | tf_op jit(solution)/shard_map/all_to_all | solution.py:96
  402.5 22.9 %copy.36 = bf16[64,8,128,256]{3,0,1,2:T(8,128)(2,1)} copy(bf16[64,8,128,256]{3,0,2,1:T(8,128)(2,1)} %bitcast.5) | data formatting | bytes 67108864 | tf_op jit(solution)/shard_map/all_to_all | solution.py:96
  425.4 53.7 %fusion.10 = f32[128,512,256]{2,1,0:T(8,128)} fusion(bf16[512,128,256]{2,0,1:T(8,128)(2,1)} %bitcast.54, bf16[128,256,512]{2,1,0:T(8,128)(2,1)} %get-tuple-element.10, bf16[128,256,512]{2,1,0:T(8,128)(2,1)} %get-tuple-element.9), kind=kOutput, calls=%fused_computation.12 | convolution fusion | flops 17314086912 | bytes 167772160 | tf_op jit(solution)/shard_map/cos,sck->cok/dot_general | solution.py:52
  479.1 26.5 %fusion.28 = (bf16[128,256,1,128]{3,1,0,2:T(8,128)(2,1)S(1)}, bf16[128,256,1,128]{3,1,0,2:T(8,128)(2,1)}) fusion(f32[128,512,256]{2,1,0:T(8,128)} %fusion.10), kind=kLoop, calls=%fused_computation.38 | loop fusion | flops 16777216 | bytes 83886080 | tf_op jit(solution)/shard_map/stack | solution.py:56
  505.6 6.2 pad_maximum_fusion.1
  511.8 36.9 %copy.37 = bf16[128,256,2,128]{3,0,2,1:T(8,128)(2,1)} copy(bf16[128,256,2,128]{3,1,0,2:T(8,128)(2,1)S(1)} %pad_maximum_fusion.1) | data formatting | bytes 33554432 | tf_op jit(solution)/shard_map/stack | solution.py:56
  548.7 5.9 all-to-all-start.1
  556.4 16.4 %fusion.73 = bf16[1024,1024,1]{1,0,2:T(8,128)(2,1)} fusion(), kind=kLoop, calls=%fused_computation.51.clone.clone.1 | loop fusion | flops 16777216 | bytes 2097152 | tf_op jit(solution)/shard_map/cn,cbk->bnk/dot_general | solution.py:64
  572.8 15.8 %fusion.75 = bf16[1024,1024,1]{1,0,2:T(8,128)(2,1)S(1)} fusion(), kind=kLoop, calls=%fused_computation.52.clone.clone.1 | loop fusion | flops 16777216 | bytes 2097152 | tf_op jit(solution)/shard_map/cn,cbk->bnk/dot_general | solution.py:67
  588.7 149.9 %all-to-all-done.1 = bf16[128,256,2,128]{3,0,2,1:T(8,128)(2,1)} async-done(((bf16[128,256,2,128]{3,0,2,1:T(8,128)(2,1)}), bf16[128,256,2,128]{3,0,2,1:T(8,128)(2,1)}, u32[]{:S(2)}, u32[]{:S(2)}) %all-to-all-start.1) | async-done | bytes 16777248 | tf_op jit(solution)/shard_map/all_to_all | solution.py:98
  738.5 23.4 %copy.38 = bf16[128,8,32,2,128]{0,1,4,3,2:T(8,128)(2,1)} copy(bf16[128,8,32,2,128]{4,0,3,2,1:T(8,128)(2,1)} %bitcast.10) | data formatting | bytes 33554432 | tf_op jit(solution)/shard_map/all_to_all | solution.py:98
  761.9 25.3 %reshape.36 = bf16[1024,32,256]{0,2,1:T(8,128)(2,1)} reshape(bf16[8,128,32,2,128]{1,0,4,3,2:T(8,128)(2,1)} %bitcast.53) | data formatting | bytes 33554432 | tf_op jit(solution)/shard_map/reshape | solution.py:63
  787.2 33.7 %fusion.22 = f32[32,1024,256]{1,0,2:T(8,128)} fusion(bf16[1024,32,256]{0,2,1:T(8,128)(2,1)} %reshape.36, bf16[1024,1024,1]{1,0,2:T(8,128)(2,1)} %fusion.73), kind=kOutput, calls=%fused_computation.36 | convolution fusion | flops 17179869184 | bytes 52428800 | tf_op jit(solution)/shard_map/cn,cbk->bnk/dot_general | solution.py:64
  820.9 33.1 %fusion.25 = f32[32,1024,256]{1,0,2:T(8,128)} fusion(bf16[1024,32,256]{0,2,1:T(8,128)(2,1)} %reshape.36, bf16[1024,1024,1]{1,0,2:T(8,128)(2,1)S(1)} %fusion.75), kind=kOutput, calls=%fused_computation.37 | convolution fusion | flops 17179869184 | bytes 52428800 | tf_op jit(solution)/shard_map/cn,cbk->bnk/dot_general | solution.py:67
  854.0 34.4 %fusion.15 = (f32[32,1024,1,128]{1,0,3,2:T(8,128)}, f32[32,1024,1,128]{1,0,3,2:T(8,128)}) fusion(f32[32,1024,256]{1,0,2:T(8,128)} %fusion.25, f32[32,1024,256]{1,0,2:T(8,128)} %fusion.22), kind=kLoop, calls=%fused_computation.25 | loop fusion | flops 8388608 | bytes 100663296 | tf_op jit(solution)/shard_map/stack | solution.py:70
  888.5 27.8 %pad_maximum_fusion = f32[32,1024,2,128]{1,0,3,2:T(8,128)} fusion(f32[32,1024,1,128]{1,0,3,2:T(8,128)} %get-tuple-element.6, f32[32,1024,1,128]{1,0,3,2:T(8,128)} %get-tuple-element.5), kind=kLoop, calls=%fused_computation.17 | loop fusion | flops 8388608 | bytes 67108864 | tf_op jit(solution)/shard_map/stack | solution.py:70
  921.2 4.3 collective-permute-start
  925.6 54.2 %multiply_add_fusion = f32[32,1024,2,128]{1,0,3,2:T(8,128)} fusion(f32[32,1024,2,128]{1,0,3,2:T(8,128)} %pad_maximum_fusion, f32[1024]{0:T(1024)S(1)} %bitcast.62, f32[1024]{0:T(1024)S(1)} %bitcast.64, f32[1024]{0:T(1024)S(1)} %bitcast.60, f32[1024]{0:T(1024)S(1)} %bitcast.66), kind=kLoop, calls=%fused_computation.20 | loop fusion | flops 58720256 | bytes 67125248 | tf_op jit(solution)/shard_map/add | solution.py:79
  979.8 12.0 %slice.148 = bf16[32,1024,2,125]{1,0,3,2:T(8,128)(2,1)S(1)} slice(f32[32,1024,2,128]{1,0,3,2:T(8,128)} %multiply_add_fusion), slice={[0:32], [0:1024], [0:2], [3:128]} | slice | bytes 32768000 | tf_op jit(solution)/shard_map/slice | solution.py:111
  993.0 7.0 pad_maximum_fusion.2
  1000.0 23.1 %copy.42 = bf16[32,1024,256]{2,1,0:T(8,128)(2,1)} copy(bf16[32,1024,256]{1,0,2:T(8,128)(2,1)} %bitcast.52) | data formatting | bytes 33554432 | tf_op jit(solution)/shard_map/convert_element_type | solution.py:113
  (37 shorter events, 9.2 us)
Async XLA Ops:
  30.6 7.6 copy-start.2
  30.6 7.8 copy-start.3
  30.6 7.9 copy-start.4
  30.6 371.9 %all-to-all-start = ((bf16[64,1024,256]{2,0,1:T(8,128)(2,1)}), bf16[64,1024,256]{2,0,1:T(8,128)(2,1)}, u32[]{:S(2)}, u32[]{:S(2)}) async-start(bf16[64,1024,256]{2,0,1:T(8,128)(2,1)} %copy_multiply_fusion), calls=%async_computation | async-start | bytes 67108864 | tf_op jit(solution)/shard_map/all_to_all | solution.py:96
  548.7 5.9 copy-start.11
  548.7 189.8 %all-to-all-start.1 = ((bf16[128,256,2,128]{3,0,2,1:T(8,128)(2,1)}), bf16[128,256,2,128]{3,0,2,1:T(8,128)(2,1)}, u32[]{:S(2)}, u32[]{:S(2)}) async-start(bf16[128,256,2,128]{3,0,2,1:T(8,128)(2,1)} %copy.37), calls=%async_computation.1 | async-start | bytes 33554432 | tf_op jit(solution)/shard_map/all_to_all | solution.py:98
  555.2 0.6 copy-start.8
  888.5 27.8 %copy-start = (f32[32,1024,1,128]{1,0,3,2:T(8,128)S(1)}, f32[32,1024,1,128]{1,0,3,2:T(8,128)}, u32[]{:S(2)}) copy-start(f32[32,1024,1,128]{1,0,3,2:T(8,128)} %get-tuple-element.5) | copy-start | bytes 50331652
  888.5 31.9 %copy-start.1 = (f32[32,1024,1,128]{1,0,3,2:T(8,128)S(1)}, f32[32,1024,1,128]{1,0,3,2:T(8,128)}, u32[]{:S(2)}) copy-start(f32[32,1024,1,128]{1,0,3,2:T(8,128)} %get-tuple-element.6) | copy-start | bytes 50331652
  920.4 0.7 copy-start.5
  920.4 0.7 copy-start.6
  920.4 0.7 copy-start.7
  920.4 0.7 copy-start.10
  920.4 5.2 copy-start.9
  921.2 70.5 %collective-permute-start = (f32[32,1024,2,3]{1,0,3,2:T(8,128)S(1)}, f32[32,1024,2,3]{1,0,3,2:T(8,128)S(1)}, u32[]{:S(2)}, u32[]{:S(2)}) collective-permute-start(f32[32,1024,2,3]{1,0,3,2:T(8,128)S(1)} %fusion.48), channel_id=1, source_target_pairs={{0,8},{8,16},{16,24},{1,9},{9,17},{17,25},{2,10},{10,18},{18,26},{... | collective-permute-start | bytes 2359304 | tf_op jit(solution)/shard_map/ppermute | solution.py:17
where the time goes:
time: 1030 us; the launch traced here: 1020 us
  other arithmetic  478 us (46%)
  waiting for transfers between devices  257 us (25%)
  local copies, waits for them, and re-layouts  150 us (15%)
  matrix products  120 us (12%)
  starting transfers between devices  17.7 us (2%)
    another operation x2, other arithmetic  258 us
    all_to_all x1, waiting for transfers between devices, per_device(): lax.all_to_all(beamed, 'chan', split_axis=1, concat_axis=0, tiled=True)  150 us
    all_to_all x1, waiting for transfers between devices, per_device(): lax.all_to_all(scaled, 'chan', split_axis=1, concat_axis=0, tiled=True)  107 us
    another operation x3, other arithmetic, synthesize(): return jnp.stack([real_part, imag_part], axis=2)  62.3 us
    add x2, other arithmetic, apply_taps(): running + filter_taps[tap_index][None, :, None, None] * extended[:, :, :,...  54.4 us
    dot_general x1, matrix products, form_beams(): jnp.einsum('cos,sck->cok', weights, flattened, preferred_element_type=jnp...  53.7 us
    another operation x1, local copies, waits for them, and re-layouts, form_beams(): return jnp.stack([real_part, imag_part], axis=2).astype(jnp.bfloat16)  36.9 us
    dot_general x1, matrix products, synthesize(): jnp.einsum('cn,cbk->bnk', cosine_table, flattened, preferred_element_type...  33.7 us
  transfers between devices with their start and end apart: 3, of which 2 were waited for; matrix products, arithmetic and copies ran while one was open for 35% of the time, Pallas kernels for 0%

commit v1 on v0

v1 whole, which is shorter than its diff:
```python
import functools
import math

import jax
import jax.numpy as jnp
from jax import lax
from jax.experimental import pallas as pl
from jax.experimental.pallas import tpu as pltpu
from jax.sharding import PartitionSpec as P


TWO_PI = 6.283185307179586
CHUNKS = 2
VMEM_LIMIT = 56 * 1024 * 1024


def radix_of(chunk_channels):
    return max(r for r in (4, 2, 1) if chunk_channels % r == 0 and (chunk_channels // r) % 16 == 0 or r == 1)


def synthesis_tables(channels, devices, chunk_channels, radix):
    span = channels // radix
    per = chunk_channels // radix
    local = CHUNKS * chunk_channels
    shape = (radix, span, span)
    residue = lax.broadcasted_iota(jnp.int32, shape, 0)
    sample = lax.broadcasted_iota(jnp.int32, shape, 1)
    place = lax.broadcasted_iota(jnp.int32, shape, 2)
    chunk = place // (devices * per)
    source = place // per % devices
    channel = source * local + chunk * chunk_channels + place % per * radix + residue
    phases = TWO_PI / channels * (channel * sample % channels).astype(jnp.float32)
    normalizer = 1.0 / math.sqrt(channels)
    cosine = (jnp.cos(phases) * normalizer).astype(jnp.bfloat16)
    sine = (jnp.sin(phases) * normalizer).astype(jnp.bfloat16)
    return jnp.concatenate([cosine, sine], axis=2)


def beam_weights(gain_real, gain_imag, delays, chan_start, channels):
    local_count = gain_real.shape[1]
    stations = delays.shape[0]
    channel = (chan_start + lax.broadcasted_iota(jnp.int32, (local_count,), 0)).astype(jnp.float32)
    frequency = (channel + 0.5) / channels - 0.5
    turns = TWO_PI * frequency
    phases = turns[:, None, None] * jnp.transpose(delays)[None, :, :]
    cosines = jnp.cos(phases)
    sines = jnp.sin(phases)
    real_gain = jnp.transpose(gain_real)[:, None, :]
    imag_gain = jnp.transpose(gain_imag)[:, None, :]
    scale_factor = 1.0 / math.sqrt(stations)
    weight_real = (real_gain * cosines + imag_gain * sines) * scale_factor
    weight_imag = (imag_gain * cosines - real_gain * sines) * scale_factor
    return weight_real.astype(jnp.bfloat16), weight_imag.astype(jnp.bfloat16)


def beam_kernel(n_taps, wr, wi, x, o, s_re, s_im, ends):
    devices, group, per_device, lanes = x.shape
    beams_local, per = o.shape[1] - 1, o.shape[2]
    beams = devices * beams_local
    half = lanes // 2
    tail = n_taps - 1
    step = pl.program_id(1)
    for j in range(group):
        block = x[:, j].reshape(devices * per_device, lanes)
        real = jnp.dot(wr[j], block, preferred_element_type=jnp.float32)
        imag = jnp.dot(wi[j], block, preferred_element_type=jnp.float32)
        rows = pl.ds(step * group + j, beams, stride=per)
        s_re[rows, :] = real[:, :half] - imag[:, half:]
        s_im[rows, :] = real[:, half:] + imag[:, :half]

    @pl.when(step == pl.num_programs(1) - 1)
    def _():
        take = math.gcd(16, beams_local)
        lane = lax.broadcasted_iota(jnp.int32, (per, half), 1)
        ends[...] = jnp.zeros_like(ends)

        def flush(i, carry):
            device = i * take // beams_local
            base = i * take % beams_local
            src = pl.ds(pl.multiple_of(i * take * per, take * per), take * per)
            for part, scratch in enumerate((s_re, s_im)):
                cols = slice(part * half, (part + 1) * half)
                found = scratch[src, :]
                o[device, pl.ds(base, take), :, cols] = found.reshape(take, per, half).astype(o.dtype)
                total = ends[device, :, cols]
                for t in range(take):
                    place = lane - n_taps * (base + t)
                    moved = pltpu.roll(found[t * per : (t + 1) * per], (n_taps * (base + t) + tail) % half, 1)
                    total = jnp.where(jnp.logical_and(place >= 0, place < tail), moved, total)
                ends[device, :, cols] = total
            return carry

        lax.fori_loop(0, beams // take, flush, 0)
        o[:, beams_local] = ends[...].astype(o.dtype)


def form_beams(weight_real, weight_imag, received, radix, n_taps):
    devices, chunk_channels, per_device, lanes = received.shape
    beams, stations = weight_real.shape[1:]
    per = chunk_channels // radix
    rooms = beams // devices + 1
    group = 4
    view = (per, radix, beams, stations)
    weight_spec = pl.BlockSpec((group, None, beams, stations), lambda r, i: (i, r, 0, 0))
    flops = 8 * chunk_channels * beams * stations * lanes // 2
    return pl.pallas_call(
        functools.partial(beam_kernel, n_taps),
        name="form_beams",
        grid=(radix, per // group),
        in_specs=[
            weight_spec,
            weight_spec,
            pl.BlockSpec((devices, group, None, per_device, lanes), lambda r, i: (0, i, r, 0, 0)),
        ],
        out_specs=pl.BlockSpec((devices, rooms, per, lanes), lambda r, i: (0, 0, r, 0)),
        out_shape=jax.ShapeDtypeStruct((devices, rooms, chunk_channels, lanes), jnp.bfloat16),
        scratch_shapes=[pltpu.VMEM((beams * per, lanes // 2), jnp.float32)] * 2
        + [pltpu.VMEM((devices, per, lanes), jnp.float32)],
        compiler_params=pltpu.CompilerParams(vmem_limit_bytes=VMEM_LIMIT),
        cost_estimate=pl.CostEstimate(
            flops=flops,
            bytes_accessed=2 * chunk_channels * (2 * beams * stations + stations * lanes + beams * lanes),
            transcendentals=0,
        ),
    )(
        weight_real.reshape(view),
        weight_imag.reshape(view),
        received.reshape(devices, per, radix, per_device, lanes),
    )


def times_unit(value, turn, radix):
    re, im = value
    quarter = turn * (4 // radix) % 4
    return ((re, im), (-im, re), (-re, -im), (im, -re))[quarter]


def combine(values, q):
    radix = len(values)
    re, im = values[0]
    for r in range(1, radix):
        more_re, more_im = times_unit(values[r], r * q, radix)
        re, im = re + more_re, im + more_im
    return re, im


def synthesis_kernel(radix, *refs):
    tab, taps, taps_masked = refs[:3]
    blocks = refs[3 : 3 + CHUNKS]
    halos = refs[3 + CHUNKS : 3 + 2 * CHUNKS]
    o, partial, before = refs[3 + 2 * CHUNKS :]
    n_taps, channels, half = taps.shape
    span = channels // radix
    rows = 16
    beam = pl.program_id(0)

    def transform(chunks, slot, r):
        per = chunks[0].shape[1] // radix
        parts = [c[:, r * per : (r + 1) * per, :].reshape(-1, 2 * half) for c in chunks]
        x = jnp.concatenate(parts, axis=0)
        turned = jnp.concatenate([-x[:, half:], x[:, :half]], axis=1)
        both = jnp.concatenate([x, turned], axis=0)
        partial[slot, r] = jnp.dot(tab[r], both, preferred_element_type=jnp.float32)

    def on_rows(start, slot, store):
        values = []
        for r in range(radix):
            both = partial[slot, r, pl.ds(start, rows), :]
            values.append((both[:, :half], both[:, half:]))
        for q in range(radix):
            store(pl.ds(q * span + start, rows), combine(values, q))

    lane = lax.broadcasted_iota(jnp.int32, (rows, half), 1)

    @pl.when(beam == 0)
    def _():
        for r in range(radix):
            transform(halos, 1, r)
        frame = lane % n_taps

        def store(at, signal):
            for part in range(2):
                total = jnp.zeros((rows, half), jnp.float32)
                for k in range(1, n_taps):
                    back = n_taps - 1 - k
                    moved = pltpu.roll(signal[part], (half - back) % half, 1) if back else signal[part]
                    total = total + jnp.where(frame < k, taps[k, at, :] * moved, 0.0)
                before[at, part * half : (part + 1) * half] = total

        def body(i, carry):
            on_rows(pl.multiple_of(i * rows, rows), 1, store)
            return carry

        lax.fori_loop(0, span // rows, body, 0)

    new, old = beam % 2, (beam + 1) % 2
    shift = (half - n_taps * jnp.maximum(beam - 1, 0)) % half

    def store(at, signal):
        for part in range(2):
            cols = slice(part * half, (part + 1) * half)
            total = taps_masked[0, at, :] * signal[part]
            for k in range(1, n_taps):
                total = total + taps_masked[k, at, :] * pltpu.roll(signal[part], k, 1)
            total = total + jnp.where(lane < n_taps - 1, pltpu.roll(before[at, cols], shift, 1), 0.0)
            o[at, cols] = total.astype(o.dtype)

    for r in range(radix):
        transform(blocks, new, r)
        for start in range(r * span // radix, (r + 1) * span // radix, rows):
            on_rows(start, old, store)


def synthesize(tables, filter_taps, spectra, halos, radix):
    devices, rooms, chunk_channels, lanes = spectra[0].shape
    beams = rooms - 1
    n_taps, channels = filter_taps.shape
    half = lanes // 2
    span = channels // radix
    taps = jnp.broadcast_to(filter_taps[:, :, None], (n_taps, channels, half))
    lane = lax.broadcasted_iota(jnp.int32, taps.shape, 2)
    masked = jnp.where(lane >= lax.broadcasted_iota(jnp.int32, taps.shape, 0), taps, 0.0)
    whole = lambda shape: pl.BlockSpec(shape, lambda b: (0,) * len(shape), pipeline_mode=pl.Buffered(1))
    return pl.pallas_call(
        functools.partial(synthesis_kernel, radix),
        name="synthesize",
        grid=(beams + 1,),
        in_specs=[whole(tables.shape), whole(taps.shape), whole(taps.shape)]
        + [pl.BlockSpec((devices, None, chunk_channels, lanes), lambda b: (0, jnp.minimum(b, beams - 1), 0, 0))] * CHUNKS
        + [whole(halos[0].shape)] * CHUNKS,
        out_specs=pl.BlockSpec((None, channels, lanes), lambda b: (jnp.maximum(b - 1, 0), 0, 0)),
        out_shape=jax.ShapeDtypeStruct((beams, channels, lanes), jnp.bfloat16),
        scratch_shapes=[
            pltpu.VMEM((2, radix, span, lanes), jnp.float32),
            pltpu.VMEM((channels, lanes), jnp.float32),
        ],
        compiler_params=pltpu.CompilerParams(vmem_limit_bytes=VMEM_LIMIT),
    )(tables, taps, masked, *spectra, *halos)


def exchange(block):
    return lax.all_to_all(block, "chan", split_axis=0, concat_axis=0, tiled=True)


def per_device(voltages, exponents, gain_real, gain_imag, delays, filter_taps):
    per_station, channels, lanes = voltages.shape
    devices = lax.axis_size("chan")
    local_count = channels // devices
    chunk_channels = local_count // CHUNKS
    radix = radix_of(chunk_channels)
    n_taps = filter_taps.shape[0]
    block_width = channels // exponents.shape[1]
    factor = jnp.repeat(jnp.exp2(exponents.astype(jnp.float32)), block_width, axis=1).astype(jnp.bfloat16)
    factor = factor.reshape(per_station, devices, CHUNKS, chunk_channels, 1)
    start = lax.axis_index("chan") * local_count
    forward = [(i, i + 1) for i in range(lax.axis_size("tm") - 1)]
    received, weights, spectra, halos = [], [], [], []
    source = voltages
    for k in range(CHUNKS):
        parts = source.reshape(per_station, devices, CHUNKS, chunk_channels, lanes)
        packed = jnp.transpose(parts[:, :, k] * factor[:, :, k], (1, 2, 0, 3))
        packed, source = lax.optimization_barrier((packed, source))
        received.append(exchange(packed))
        mine = slice(k * chunk_channels, (k + 1) * chunk_channels)
        first = start + k * chunk_channels
        pair = beam_weights(gain_real[:, mine], gain_imag[:, mine], delays, first, channels)
        held = (pair, delays, gain_real, gain_imag, start)
        pair, delays, gain_real, gain_imag, start = lax.optimization_barrier(held)
        weights.append(pair)
    tables = synthesis_tables(channels, devices, chunk_channels, radix)
    for k in range(CHUNKS):
        beamed = form_beams(*weights[k], received[k], radix, n_taps)
        spectra.append(exchange(beamed))
    for k in range(CHUNKS):
        halos.append(lax.ppermute(spectra[k][:, -1], "tm", forward))
    return synthesize(tables, filter_taps, spectra, halos, radix)


def solution(mesh):
    placed = (
        P("chan", None, "tm"),
        P("chan", None, "tm"),
        P(None, "chan"),
        P(None, "chan"),
        P(),
        P(),
    )

    return jax.shard_map(per_device, mesh=mesh, in_specs=placed, out_specs=P("chan", None, "tm"), check_vma=False)
```

time: 1030 us -> 745 us (0.72)
  other arithmetic: 478 us -> 289 us
  Pallas kernels: 0 us -> 134 us
  local copies, waits for them, and re-layouts: 150 us -> 21.2 us
  matrix products: 120 us -> 0 us
  starting transfers between devices: 17.7 us -> 30.7 us
  waiting for transfers between devices: 257 us -> 269 us
    another operation x7 -> x0, other arithmetic: 353 us -> none
    convert_element_type x0 -> x3, other arithmetic: none -> 263 us  [the longest x2 259 us: beam_weights(): return (weight_real.astype(jnp.bfloat16), weight_imag.astype(jnp.bfloat16))]
    pallas_call x0 -> x3, Pallas kernels: none -> 134 us  [the longest x2 75.2 us: form_beams(): pl.pallas_call(functools.partial(beam_kernel, n_taps), name='form_beams',...]
    dot_general x3 -> x0, matrix products: 120 us -> none  [the longest x1 53.7 us: form_beams(): jnp.einsum('cos,sck->cok', weights, flattened, preferred_element_type=jnp...]
    add x2 -> x0, other arithmetic: 54.4 us -> none  [apply_taps(): running + filter_taps[tap_index][None, :, None, None] * extended[:, :, :,...]
    all_to_all x2 -> x0, local copies, waits for them, and re-layouts: 46.3 us -> none  [the longest x1 23.4 us: per_device(): lax.all_to_all(beamed, 'chan', split_axis=1, concat_axis=0, tiled=True)]
    another operation x1 -> x0, local copies, waits for them, and re-layouts: 36.9 us -> none  [form_beams(): return jnp.stack([real_part, imag_part], axis=2).astype(jnp.bfloat16)]
    dot_general x2 -> x0, other arithmetic: 32.3 us -> none  [the longest x1 16.4 us: synthesize(): jnp.einsum('cn,cbk->bnk', cosine_table, flattened, preferred_element_type...]
  transfers between devices with their start and end apart: 3 -> 6, of which waited for: 2 -> 4; matrix products, arithmetic and copies ran while one was open for 35% -> 39% of each run, Pallas kernels for 0% -> 10%
where the time goes in v1:
time: 745 us; the launch traced here: 744 us
  other arithmetic  289 us (39%)
  waiting for transfers between devices  269 us (36%)
  Pallas kernels  134 us (18%)
  starting transfers between devices  30.7 us (4%)
  local copies, waits for them, and re-layouts  21.2 us (3%)
    all_to_all x4, waiting for transfers between devices, exchange(): lax.all_to_all(block, 'chan', split_axis=0, concat_axis=0, tiled=True)  268 us
    convert_element_type x2, other arithmetic, beam_weights(): return (weight_real.astype(jnp.bfloat16), weight_imag.astype(jnp.bfloat16))  259 us
    pallas_call x2, Pallas kernels, form_beams(): pl.pallas_call(functools.partial(beam_kernel, n_taps), name='form_beams',...  75.2 us
    pallas_call x1, Pallas kernels, synthesize(): pl.pallas_call(functools.partial(synthesis_kernel, radix), name='synthesi...  58.4 us
    transpose x2, other arithmetic, per_device(): packed = jnp.transpose(parts[:, :, k] * factor[:, :, k], (1, 2, 0, 3))  22.3 us
    all_to_all x4, starting transfers between devices, exchange(): lax.all_to_all(block, 'chan', split_axis=0, concat_axis=0, tiled=True)  22 us
    slice x3, local copies, waits for them, and re-layouts, per_device(): packed = jnp.transpose(parts[:, :, k] * factor[:, :, k], (1, 2, 0, 3))  16.2 us
  transfers between devices with their start and end apart: 6, of which 4 were waited for; matrix products, arithmetic and copies ran while one was open for 39% of the time, Pallas kernels for 10%

profile of v1, /device:TPU:0, one launch (start us, length us, event | category | flops | bytes accessed | tf_op | source)
XLA Modules:
  0.0 744.2 jit_solution(2477178771935651999)
XLA Ops:
  0.7 8.1 %slice.48 = bf16[64,8,1,64,256]{4,3,2,1,0:T(8,128)(2,1)S(1)} slice(bf16[64,8,2,64,256]{4,3,2,1,0:T(8,128)(2,1)} %bitcast.52), slice={[0:64], [0:8], [0:1], [0:64], [0:256]} | slice | bytes 33554432 | tf_op jit(solution)/shard_map/slice | solution.py:261
  8.8 11.1 %fusion.23 = bf16[8,64,64,256]{3,2,1,0:T(8,128)(2,1)} fusion(bf16[64,8,1,64,256]{4,3,2,1,0:T(8,128)(2,1)S(1)} %slice.48, bf16[64,8]{0,1:T(8,128)(2,1)S(1)} %get-tuple-element.46), kind=kLoop, calls=%fused_computation.29 | loop fusion | flops 8388608 | bytes 33555456 | tf_op jit(solution)/shard_map/transpose | solution.py:261
  19.9 5.7 all-to-all-start
  25.6 8.1 %slice.50 = bf16[64,8,1,64,256]{4,3,2,1,0:T(8,128)(2,1)S(1)} slice(bf16[64,8,2,64,256]{4,3,2,1,0:T(8,128)(2,1)} %bitcast.53), slice={[0:64], [0:8], [1:2], [0:64], [0:256]} | slice | bytes 33554432 | tf_op jit(solution)/shard_map/slice | solution.py:261
  33.7 11.2 %fusion.21 = bf16[8,64,64,256]{3,2,1,0:T(8,128)(2,1)} fusion(bf16[64,8,1,64,256]{4,3,2,1,0:T(8,128)(2,1)S(1)} %slice.50, bf16[64,8]{0,1:T(8,128)(2,1)S(1)} %get-tuple-element.45), kind=kLoop, calls=%fused_computation.26 | loop fusion | flops 8388608 | bytes 33555456 | tf_op jit(solution)/shard_map/transpose | solution.py:261
  44.9 165.3 %all-to-all-done = bf16[8,64,64,256]{3,2,1,0:T(8,128)(2,1)} async-done(((bf16[8,64,64,256]{3,2,1,0:T(8,128)(2,1)}), bf16[8,64,64,256]{3,2,1,0:T(8,128)(2,1)}, u32[]{:S(2)}, u32[]{:S(2)}) %all-to-all-start) | async-done | bytes 16777248 | tf_op jit(solution)/shard_map/all_to_all | solution.py:242
  210.3 5.9 all-to-all-start.2
  216.8 129.3 %fusion.19 = (bf16[64,256,512]{2,1,0:T(8,128)(2,1)}, bf16[64,256,512]{2,1,0:T(8,128)(2,1)}) fusion(f32[64,512]{1,0:T(8,128)S(1)} %copy.46, f32[256,512]{1,0:T(8,128)S(1)} %copy.45, f32[64]{0:T(128)S(1)} %add_multiply_fusion.1, f32[64,512]{1,0:T(8,128)S(1)} %copy.44), kind=kLoop, calls=%fused_computation.23 | loop fusion | flops 92274688 | bytes 34341120 | tf_op jit(solution)/shard_map/convert_element_type | solution.py:53
  346.1 37.6 %form_beams.2 = bf16[8,33,64,256]{3,2,1,0:T(8,128)(2,1)} custom-call(bf16[16,4,256,512]{3,2,1,0:T(8,128)(2,1)} %bitcast.49, bf16[16,4,256,512]{3,2,1,0:T(8,128)(2,1)} %bitcast.48, bf16[8,16,4,64,256]{4,3,2,1,0:T(8,128)(2,1)} %bitcast.10.x), custom_call_target="tpu_custom_call" | custom-call | flops 8589934592 | bytes 58720256 | tf_op jit(solution)/shard_map/form_beams/pallas_call | solution.py:106
  383.7 16.3 %all-to-all-done.2 = bf16[8,64,64,256]{3,2,1,0:T(8,128)(2,1)} async-done(((bf16[8,64,64,256]{3,2,1,0:T(8,128)(2,1)}), bf16[8,64,64,256]{3,2,1,0:T(8,128)(2,1)}, u32[]{:S(2)}, u32[]{:S(2)}) %all-to-all-start.2) | async-done | bytes 16777248 | tf_op jit(solution)/shard_map/all_to_all | solution.py:242
  400.0 5.2 all-to-all-start.1
  405.8 129.3 %fusion.13 = (bf16[64,256,512]{2,1,0:T(8,128)(2,1)}, bf16[64,256,512]{2,1,0:T(8,128)(2,1)}) fusion(f32[64,512]{1,0:T(8,128)S(1)} %copy.51, f32[256,512]{1,0:T(8,128)S(1)} %copy.50, f32[64]{0:T(128)S(1)} %add_multiply_fusion, f32[64,512]{1,0:T(8,128)S(1)} %copy.49), kind=kLoop, calls=%fused_computation.17 | loop fusion | flops 92274688 | bytes 34341120 | tf_op jit(solution)/shard_map/convert_element_type | solution.py:53
  535.2 37.6 %form_beams.3 = bf16[8,33,64,256]{3,2,1,0:T(8,128)(2,1)} custom-call(bf16[16,4,256,512]{3,2,1,0:T(8,128)(2,1)} %bitcast.51, bf16[16,4,256,512]{3,2,1,0:T(8,128)(2,1)} %bitcast.50, bf16[8,16,4,64,256]{4,3,2,1,0:T(8,128)(2,1)} %bitcast.19.x), custom_call_target="tpu_custom_call" | custom-call | flops 8589934592 | bytes 58720256 | tf_op jit(solution)/shard_map/form_beams/pallas_call | solution.py:106
  572.8 5.1 all-to-all-start.3
  578.0 4.4 multiply_convert_fusion.1
  582.4 1.1 pad_maximum_fusion.refs_0_
  584.4 4.2 collective-permute-start
  588.6 86.1 %all-to-all-done.3.refs_4_ = bf16[8,33,64,256]{3,2,1,0:T(8,128)(2,1)} async-done(((bf16[8,33,64,256]{3,2,1,0:T(8,128)(2,1)}), bf16[8,33,64,256]{3,2,1,0:T(8,128)(2,1)}, u32[]{:S(2)}, u32[]{:S(2)}) %all-to-all-start.3) | async-done | bytes 8650784 | tf_op jit(solution)/shard_map/all_to_all | solution.py:242
  674.8 1.0 slice_bitcast_fusion
  675.7 4.5 collective-permute-start.1
  680.3 2.0 fusion.24.refs_2_
  682.2 1.6 collective-permute-done.1.refs_6_
  683.8 2.0 broadcast_in_dim.5.refs_1_
  685.8 58.4 %synthesize.1 = bf16[32,1024,256]{2,1,0:T(8,128)(2,1)} custom-call(bf16[4,256,512]{2,1,0:T(8,128)(2,1)} %pad_maximum_fusion.refs_0_, f32[4,1024,128]{2,1,0:T(8,128)} %broadcast_in_dim.5.refs_1_, f32[4,1024,128]{2,1,0:T(8,128)} %fusion.24.refs_2_, bf16[8,33,64,256]{3,2,1,0:T(8,128)(2,1)} %all-to-all-done.1.refs_3_, ...), custom_call_target="tpu_custom_call" | custom-call | tf_op jit(solution)/shard_map/synthesize/pallas_call | solution.py:224
  (34 shorter events, 2.8 us)
Async XLA Ops:
  19.9 190.4 %all-to-all-start = ((bf16[8,64,64,256]{3,2,1,0:T(8,128)(2,1)}), bf16[8,64,64,256]{3,2,1,0:T(8,128)(2,1)}, u32[]{:S(2)}, u32[]{:S(2)}) async-start(bf16[8,64,64,256]{3,2,1,0:T(8,128)(2,1)} %fusion.23), calls=%async_computation | async-start | bytes 33554432 | tf_op jit(solution)/shard_map/all_to_all | solution.py:242
  44.9 171.3 %copy-start.2 = (f32[512,128]{1,0:T(8,128)S(1)}, f32[512,128]{1,0:T(8,128)}, u32[]{:S(2)}) copy-start(f32[512,128]{1,0:T(8,128)} %param.8) | copy-start | bytes 786436
  44.9 171.4 %copy-start.1 = (f32[512,128]{1,0:T(8,128)S(1)}, f32[512,128]{1,0:T(8,128)}, u32[]{:S(2)}) copy-start(f32[512,128]{1,0:T(8,128)} %param.9) | copy-start | bytes 786436
  44.9 171.6 %copy-start = (f32[512,256]{1,0:T(8,128)S(1)}, f32[512,256]{1,0:T(8,128)}, u32[]{:S(2)}) copy-start(f32[512,256]{1,0:T(8,128)} %param.10) | copy-start | bytes 1572868
  210.3 189.7 %all-to-all-start.2 = ((bf16[8,64,64,256]{3,2,1,0:T(8,128)(2,1)}), bf16[8,64,64,256]{3,2,1,0:T(8,128)(2,1)}, u32[]{:S(2)}, u32[]{:S(2)}) async-start(bf16[8,64,64,256]{3,2,1,0:T(8,128)(2,1)} %fusion.21), calls=%async_computation.2 | async-start | bytes 33554432 | tf_op jit(solution)/shard_map/all_to_all | solution.py:242
  400.0 172.8 %all-to-all-start.1 = ((bf16[8,33,64,256]{3,2,1,0:T(8,128)(2,1)}), bf16[8,33,64,256]{3,2,1,0:T(8,128)(2,1)}, u32[]{:S(2)}, u32[]{:S(2)}) async-start(bf16[8,33,64,256]{3,2,1,0:T(8,128)(2,1)} %form_beams.2), calls=%async_computation.1 | async-start | bytes 17301504 | tf_op jit(solution)/shard_map/all_to_all | solution.py:242
  572.8 107.5 %copy-start.5 = (f32[4,1024]{1,0:T(4,128)S(1)}, f32[4,1024]{1,0:T(4,128)}, u32[]{:S(2)}) copy-start(f32[4,1024]{1,0:T(4,128)} %param.11) | copy-start | bytes 49156
  572.8 102.0 %all-to-all-start.3 = ((bf16[8,33,64,256]{3,2,1,0:T(8,128)(2,1)}), bf16[8,33,64,256]{3,2,1,0:T(8,128)(2,1)}, u32[]{:S(2)}, u32[]{:S(2)}) async-start(bf16[8,33,64,256]{3,2,1,0:T(8,128)(2,1)} %form_beams.3), calls=%async_computation.3 | async-start | bytes 17301504 | tf_op jit(solution)/shard_map/all_to_all | solution.py:242
  584.4 97.8 %collective-permute-start = (bf16[8,64,256]{2,1,0:T(8,128)(2,1)S(1)}, bf16[8,64,256]{2,1,0:T(8,128)(2,1)S(1)}, u32[]{:S(2)}, u32[]{:S(2)}) collective-permute-start(bf16[8,64,256]{2,1,0:T(8,128)(2,1)S(1)} %slice_bitcast_fusion.1), channel_id=1, source_target_pairs={{0,8},{8,16},{16,24},{1,9},{9,17},{17,25},{2,10},{10,18},{18,26},{... | collective-permute-start | bytes 786440 | tf_op jit(solution)/shard_map/ppermute | solution.py:275
  675.7 8.1 %collective-permute-start.1 = (bf16[8,64,256]{2,1,0:T(8,128)(2,1)S(1)}, bf16[8,64,256]{2,1,0:T(8,128)(2,1)S(1)}, u32[]{:S(2)}, u32[]{:S(2)}) collective-permute-start(bf16[8,64,256]{2,1,0:T(8,128)(2,1)S(1)} %slice_bitcast_fusion), channel_id=1, source_target_pairs={{0,8},{8,16},{16,24},{1,9},{9,17},{17,25},{2,10},{10,18},{18,26},{... | collective-permute-start | bytes 786440 | tf_op jit(solution)/shard_map/ppermute | solution.py:275
  682.2 3.6 copy-start.3
  683.8 2.0 copy-start.4

commit v2 on v1

--- a/solution.py
+++ b/solution.py
@@ -6,6 +6,7 @@
 from jax import lax
 from jax.experimental import pallas as pl
 from jax.experimental.pallas import tpu as pltpu
+from jax.experimental.layout import Layout, with_layout_constraint
 from jax.sharding import PartitionSpec as P
 
 
@@ -145,11 +146,11 @@
 
 
 def synthesis_kernel(radix, *refs):
-    tab, taps, taps_masked = refs[:3]
-    blocks = refs[3 : 3 + CHUNKS]
-    halos = refs[3 + CHUNKS : 3 + 2 * CHUNKS]
-    o, partial, before = refs[3 + 2 * CHUNKS :]
-    n_taps, channels, half = taps.shape
+    tab, taps_masked = refs[:2]
+    blocks = refs[2 : 2 + CHUNKS]
+    halos = refs[2 + CHUNKS : 2 + 2 * CHUNKS]
+    o, partial, before = refs[2 + 2 * CHUNKS :]
+    n_taps, channels, half = taps_masked.shape
     span = channels // radix
     rows = 16
     beam = pl.program_id(0)
@@ -184,7 +185,8 @@
                 for k in range(1, n_taps):
                     back = n_taps - 1 - k
                     moved = pltpu.roll(signal[part], (half - back) % half, 1) if back else signal[part]
-                    total = total + jnp.where(frame < k, taps[k, at, :] * moved, 0.0)
+                    tap = jnp.broadcast_to(taps_masked[k, at, :][:, half - 1 :], (rows, half))
+                    total = total + jnp.where(frame < k, tap * moved, 0.0)
                 before[at, part * half : (part + 1) * half] = total
 
         def body(i, carry):
@@ -225,7 +227,7 @@
         functools.partial(synthesis_kernel, radix),
         name="synthesize",
         grid=(beams + 1,),
-        in_specs=[whole(tables.shape), whole(taps.shape), whole(taps.shape)]
+        in_specs=[whole(tables.shape), whole(taps.shape)]
         + [pl.BlockSpec((devices, None, chunk_channels, lanes), lambda b: (0, jnp.minimum(b, beams - 1), 0, 0))] * CHUNKS
         + [whole(halos[0].shape)] * CHUNKS,
         out_specs=pl.BlockSpec((None, channels, lanes), lambda b: (jnp.maximum(b - 1, 0), 0, 0)),
@@ -235,7 +237,7 @@
             pltpu.VMEM((channels, lanes), jnp.float32),
         ],
         compiler_params=pltpu.CompilerParams(vmem_limit_bytes=VMEM_LIMIT),
-    )(tables, taps, masked, *spectra, *halos)
+    )(tables, masked, *spectra, *halos)
 
 
 def exchange(block):
@@ -258,9 +260,11 @@
     source = voltages
     for k in range(CHUNKS):
         parts = source.reshape(per_station, devices, CHUNKS, chunk_channels, lanes)
-        packed = jnp.transpose(parts[:, :, k] * factor[:, :, k], (1, 2, 0, 3))
+        packed = jnp.transpose(parts[:, :, k] * factor[:, :, k], (1, 0, 2, 3))
+        packed = with_layout_constraint(packed, Layout(major_to_minor=(0, 1, 2, 3)))
         packed, source = lax.optimization_barrier((packed, source))
-        received.append(exchange(packed))
+        landed = with_layout_constraint(exchange(packed), Layout(major_to_minor=(0, 1, 2, 3)))
+        received.append(jnp.transpose(landed, (0, 2, 1, 3)))
         mine = slice(k * chunk_channels, (k + 1) * chunk_channels)
         first = start + k * chunk_channels
         pair = beam_weights(gain_real[:, mine], gain_imag[:, mine], delays, first, channels)

time: 745 us -> 759 us (1.019)
  local copies, waits for them, and re-layouts: 21.2 us -> 39.5 us
  waiting for transfers between devices: 269 us -> 258 us
    transpose x0 -> x2, local copies, waits for them, and re-layouts: none -> 35.7 us  [per_device(): received.append(jnp.transpose(landed, (0, 2, 1, 3)))]
    slice x3 -> x2, local copies, waits for them, and re-layouts: 16.2 us -> 0.02 us  [per_device(): packed = jnp.transpose(parts[:, :, k] * factor[:, :, k], (1, 0, 2, 3))]
    all_to_all x4, waiting for transfers between devices: 268 us -> 256 us  [exchange(): lax.all_to_all(block, 'chan', split_axis=0, concat_axis=0, tiled=True)]
  transfers between devices with their start and end apart: 6 -> 6, of which waited for: 4 -> 3; matrix products, arithmetic and copies ran while one was open for 39% -> 42% of each run, Pallas kernels for 10% -> 10%
where the time goes in v2:
time: 759 us; the launch traced here: 758 us
  other arithmetic  296 us (39%)
  waiting for transfers between devices  258 us (34%)
  Pallas kernels  134 us (18%)
  local copies, waits for them, and re-layouts  39.5 us (5%)
  starting transfers between devices  30.4 us (4%)
    convert_element_type x2, other arithmetic, beam_weights(): return (weight_real.astype(jnp.bfloat16), weight_imag.astype(jnp.bfloat16))  259 us
    all_to_all x4, waiting for transfers between devices, exchange(): lax.all_to_all(block, 'chan', split_axis=0, concat_axis=0, tiled=True)  256 us
    pallas_call x2, Pallas kernels, form_beams(): pl.pallas_call(functools.partial(beam_kernel, n_taps), name='form_beams',...  75.2 us
    pallas_call x1, Pallas kernels, synthesize(): pl.pallas_call(functools.partial(synthesis_kernel, radix), name='synthesi...  58.4 us
    transpose x2, local copies, waits for them, and re-layouts, per_device(): received.append(jnp.transpose(landed, (0, 2, 1, 3)))  35.7 us
    transpose x2, other arithmetic, per_device(): packed = jnp.transpose(parts[:, :, k] * factor[:, :, k], (1, 0, 2, 3))  29.6 us
    all_to_all x4, starting transfers between devices, exchange(): lax.all_to_all(block, 'chan', split_axis=0, concat_axis=0, tiled=True)  21.9 us
  transfers between devices with their start and end apart: 6, of which 3 were waited for; matrix products, arithmetic and copies ran while one was open for 42% of the time, Pallas kernels for 10%

profile of v2, /device:TPU:0, one launch (start us, length us, event | category | flops | bytes accessed | tf_op | source)
XLA Modules:
  0.0 757.8 jit_solution(5255141958963161937)
XLA Ops:
  0.0 0.7 exponential_convert_fusion
  0.8 14.8 %fusion.23 = bf16[8,64,64,256]{3,2,1,0:T(8,128)(2,1)} fusion(bf16[64,8]{0,1:T(8,128)(2,1)S(1)} %get-tuple-element.46, bf16[64,8,2,64,256]{4,3,2,1,0:T(8,128)(2,1)} %bitcast.55), kind=kLoop, calls=%fused_computation.29 | loop fusion | flops 33554432 | bytes 33555456 | tf_op jit(solution)/shard_map/transpose | solution.py:263
  15.5 5.7 all-to-all-start
  21.3 14.8 %fusion.21 = bf16[8,64,64,256]{3,2,1,0:T(8,128)(2,1)} fusion(bf16[64,8]{0,1:T(8,128)(2,1)S(1)} %get-tuple-element.45, bf16[64,8,2,64,256]{4,3,2,1,0:T(8,128)(2,1)} %bitcast.56), kind=kLoop, calls=%fused_computation.26 | loop fusion | flops 33554432 | bytes 33555456 | tf_op jit(solution)/shard_map/transpose | solution.py:263
  36.1 169.8 %all-to-all-done = bf16[8,64,64,256]{3,2,1,0:T(8,128)(2,1)} async-done(((bf16[8,64,64,256]{3,2,1,0:T(8,128)(2,1)}), bf16[8,64,64,256]{3,2,1,0:T(8,128)(2,1)}, u32[]{:S(2)}, u32[]{:S(2)}) %all-to-all-start) | async-done | bytes 16777248 | tf_op jit(solution)/shard_map/all_to_all | solution.py:244
  205.9 5.7 all-to-all-start.2
  212.2 129.3 %fusion.19 = (bf16[64,256,512]{2,1,0:T(8,128)(2,1)}, bf16[64,256,512]{2,1,0:T(8,128)(2,1)}) fusion(f32[64,512]{1,0:T(8,128)S(1)} %copy.39, f32[256,512]{1,0:T(8,128)S(1)} %copy.38, f32[64]{0:T(128)S(1)} %add_multiply_fusion.1, f32[64,512]{1,0:T(8,128)S(1)} %copy.37), kind=kLoop, calls=%fused_computation.23 | loop fusion | flops 92274688 | bytes 34341120 | tf_op jit(solution)/shard_map/convert_element_type | solution.py:54
  341.5 17.8 %copy.42 = bf16[8,64,64,256]{3,2,1,0:T(8,128)(2,1)} copy(bf16[8,64,64,256]{3,1,2,0:T(8,128)(2,1)} %bitcast.9) | data formatting | bytes 33554432 | tf_op jit(solution)/shard_map/transpose | solution.py:267
  359.3 37.6 %form_beams.2 = bf16[8,33,64,256]{3,2,1,0:T(8,128)(2,1)} custom-call(bf16[16,4,256,512]{3,2,1,0:T(8,128)(2,1)} %bitcast.50, bf16[16,4,256,512]{3,2,1,0:T(8,128)(2,1)} %bitcast.49, bf16[8,16,4,64,256]{4,3,2,1,0:T(8,128)(2,1)} %bitcast.53), custom_call_target="tpu_custom_call" | custom-call | flops 8589934592 | bytes 58720256 | tf_op jit(solution)/shard_map/form_beams/pallas_call | solution.py:107
  396.9 5.2 all-to-all-start.1
  402.8 129.3 %fusion.13 = (bf16[64,256,512]{2,1,0:T(8,128)(2,1)}, bf16[64,256,512]{2,1,0:T(8,128)(2,1)}) fusion(f32[64,512]{1,0:T(8,128)S(1)} %copy.45, f32[256,512]{1,0:T(8,128)S(1)} %copy.44, f32[64]{0:T(128)S(1)} %add_multiply_fusion, f32[64,512]{1,0:T(8,128)S(1)} %copy.43), kind=kLoop, calls=%fused_computation.17 | loop fusion | flops 92274688 | bytes 34341120 | tf_op jit(solution)/shard_map/convert_element_type | solution.py:54
  532.1 17.9 %copy.48 = bf16[8,64,64,256]{3,2,1,0:T(8,128)(2,1)} copy(bf16[8,64,64,256]{3,1,2,0:T(8,128)(2,1)} %bitcast.20) | data formatting | bytes 33554432 | tf_op jit(solution)/shard_map/transpose | solution.py:267
  550.0 37.6 %form_beams.3 = bf16[8,33,64,256]{3,2,1,0:T(8,128)(2,1)} custom-call(bf16[16,4,256,512]{3,2,1,0:T(8,128)(2,1)} %bitcast.52, bf16[16,4,256,512]{3,2,1,0:T(8,128)(2,1)} %bitcast.51, bf16[8,16,4,64,256]{4,3,2,1,0:T(8,128)(2,1)} %bitcast.54), custom_call_target="tpu_custom_call" | custom-call | flops 8589934592 | bytes 58720256 | tf_op jit(solution)/shard_map/form_beams/pallas_call | solution.py:107
  587.6 5.2 all-to-all-start.3
  592.9 4.4 multiply_convert_fusion.1
  597.3 1.1 pad_maximum_fusion.refs_0_
  598.3 1.0 slice_bitcast_fusion.1
  599.3 4.2 collective-permute-start
  603.5 86.1 %all-to-all-done.3.refs_3_ = bf16[8,33,64,256]{3,2,1,0:T(8,128)(2,1)} async-done(((bf16[8,33,64,256]{3,2,1,0:T(8,128)(2,1)}), bf16[8,33,64,256]{3,2,1,0:T(8,128)(2,1)}, u32[]{:S(2)}, u32[]{:S(2)}) %all-to-all-start.3) | async-done | bytes 8650784 | tf_op jit(solution)/shard_map/all_to_all | solution.py:244
  689.6 1.0 slice_bitcast_fusion
  690.6 4.2 collective-permute-start.1
  694.8 2.0 fusion.24.refs_1_
  696.8 1.9 collective-permute-done.1.refs_5_
  699.4 58.4 %synthesize.1 = bf16[32,1024,256]{2,1,0:T(8,128)(2,1)} custom-call(bf16[4,256,512]{2,1,0:T(8,128)(2,1)} %pad_maximum_fusion.refs_0_, f32[4,1024,128]{2,1,0:T(8,128)} %fusion.24.refs_1_, bf16[8,33,64,256]{3,2,1,0:T(8,128)(2,1)} %all-to-all-done.1.refs_2_, bf16[8,33,64,256]{3,2,1,0:T(8,128)(2,1)} %all-to-all-done.3.refs_3_, bf16[8,64,256]{2,1,0:T(8,128)(2,1)} %copy-done.3, ...), custom_call_target="tpu_custom_call" | custom-call | tf_op jit(solution)/shard_map/synthesize/pallas_call | solution.py:226
  (34 shorter events, 1.9 us)
Async XLA Ops:
  15.5 190.4 %all-to-all-start = ((bf16[8,64,64,256]{3,2,1,0:T(8,128)(2,1)}), bf16[8,64,64,256]{3,2,1,0:T(8,128)(2,1)}, u32[]{:S(2)}, u32[]{:S(2)}) async-start(bf16[8,64,64,256]{3,2,1,0:T(8,128)(2,1)} %fusion.23), calls=%async_computation | async-start | bytes 33554432 | tf_op jit(solution)/shard_map/all_to_all | solution.py:244
  21.2 190.4 %copy-start.2 = (f32[512,128]{1,0:T(8,128)S(1)}, f32[512,128]{1,0:T(8,128)}, u32[]{:S(2)}) copy-start(f32[512,128]{1,0:T(8,128)} %param.8) | copy-start | bytes 786436
  21.3 190.5 %copy-start.1 = (f32[512,128]{1,0:T(8,128)S(1)}, f32[512,128]{1,0:T(8,128)}, u32[]{:S(2)}) copy-start(f32[512,128]{1,0:T(8,128)} %param.9) | copy-start | bytes 786436
  21.3 190.7 %copy-start = (f32[512,256]{1,0:T(8,128)S(1)}, f32[512,256]{1,0:T(8,128)}, u32[]{:S(2)}) copy-start(f32[512,256]{1,0:T(8,128)} %param.10) | copy-start | bytes 1572868
  205.9 191.0 %all-to-all-start.2 = ((bf16[8,64,64,256]{3,2,1,0:T(8,128)(2,1)}), bf16[8,64,64,256]{3,2,1,0:T(8,128)(2,1)}, u32[]{:S(2)}, u32[]{:S(2)}) async-start(bf16[8,64,64,256]{3,2,1,0:T(8,128)(2,1)} %fusion.21), calls=%async_computation.2 | async-start | bytes 33554432 | tf_op jit(solution)/shard_map/all_to_all | solution.py:244
  396.9 190.6 %all-to-all-start.1 = ((bf16[8,33,64,256]{3,2,1,0:T(8,128)(2,1)}), bf16[8,33,64,256]{3,2,1,0:T(8,128)(2,1)}, u32[]{:S(2)}, u32[]{:S(2)}) async-start(bf16[8,33,64,256]{3,2,1,0:T(8,128)(2,1)} %form_beams.2), calls=%async_computation.1 | async-start | bytes 17301504 | tf_op jit(solution)/shard_map/all_to_all | solution.py:244
  550.0 144.8 %copy-start.5 = (f32[4,1024]{1,0:T(4,128)S(1)}, f32[4,1024]{1,0:T(4,128)}, u32[]{:S(2)}) copy-start(f32[4,1024]{1,0:T(4,128)} %param.11) | copy-start | bytes 49156
  587.6 102.0 %all-to-all-start.3 = ((bf16[8,33,64,256]{3,2,1,0:T(8,128)(2,1)}), bf16[8,33,64,256]{3,2,1,0:T(8,128)(2,1)}, u32[]{:S(2)}, u32[]{:S(2)}) async-start(bf16[8,33,64,256]{3,2,1,0:T(8,128)(2,1)} %form_beams.3), calls=%async_computation.3 | async-start | bytes 17301504 | tf_op jit(solution)/shard_map/all_to_all | solution.py:244
  599.3 97.5 %collective-permute-start = (bf16[8,64,256]{2,1,0:T(8,128)(2,1)S(1)}, bf16[8,64,256]{2,1,0:T(8,128)(2,1)S(1)}, u32[]{:S(2)}, u32[]{:S(2)}) collective-permute-start(bf16[8,64,256]{2,1,0:T(8,128)(2,1)S(1)} %slice_bitcast_fusion.1), channel_id=1, source_target_pairs={{0,8},{8,16},{16,24},{1,9},{9,17},{17,25},{2,10},{10,18},{18,26},{... | collective-permute-start | bytes 786440 | tf_op jit(solution)/shard_map/ppermute | solution.py:279
  690.6 8.1 %collective-permute-start.1 = (bf16[8,64,256]{2,1,0:T(8,128)(2,1)S(1)}, bf16[8,64,256]{2,1,0:T(8,128)(2,1)S(1)}, u32[]{:S(2)}, u32[]{:S(2)}) collective-permute-start(bf16[8,64,256]{2,1,0:T(8,128)(2,1)S(1)} %slice_bitcast_fusion), channel_id=1, source_target_pairs={{0,8},{8,16},{16,24},{1,9},{9,17},{17,25},{2,10},{10,18},{18,26},{... | collective-permute-start | bytes 786440 | tf_op jit(solution)/shard_map/ppermute | solution.py:279
  696.8 1.9 copy-start.3
  698.7 0.7 copy-start.4
